TPU v7x, 32 devices: a whole 2x2x4 slice. The times are simulated.
32 devices in a mesh: prow: 16 (over z, y, x), pcol: 2 (over core).
Axes of the slice: x: 2, y: 2, z: 4, core: 2. Of those that a mesh axis runs over, the one named last changes fastest.
Arguments:
- right_sides: float32 [32, 1, 4096], P(None, None, 'prow'), may hold values from -6 to 6
- factor: bfloat16 [1, 4096, 8, 512], P(None, 'prow', None, 'pcol'), as said below
- node_sizes: int32 [7], replicated, may hold values from 1 to 9, 16 in all
- row_blocks: int32 [7, 16], replicated, may hold values 0 or 1
Outputs:
- forward: float32 [32, 1, 4096], P(None, None, 'prow')
- solution: float32 [32, 8, 512], P(None, None, 'pcol')
Inputs may be any that keep to these rules, and one draw needn't show every extreme that they name: factor is zero above its diagonal; its diagonal lies between 0.5 and 1. `row_blocks`: flags of tiles that belong to no proper ancestor of the supernode are ignored.
All inputs are finite; a program needn't handle non-finite values.
Results may differ from a plain program's by a relative error of at most 0.0047.
Values may be sent and summed in bfloat16 or wider, within the bound.
A program may use at most 64 MiB of HBM per device.

v0:
```python
import jax
import jax.numpy as jnp
from jax import lax
from jax.sharding import PartitionSpec as P

LEVELS = 3


def tree_tables(node_sizes, row_blocks):
    node_count = node_sizes.shape[0]
    tile_count = row_blocks.shape[1]
    tile_ends = jnp.cumsum(node_sizes)
    tile_ids = jnp.arange(tile_count, dtype=jnp.int32)
    node_of = jnp.sum((tile_ends[None, :] <= tile_ids[:, None]).astype(jnp.int32), axis=1)
    heap_label = node_count - jnp.arange(node_count, dtype=jnp.int32)
    node_depth = jnp.zeros((node_count,), jnp.int32)
    for exponent in range(1, LEVELS):
        node_depth = node_depth + (heap_label >= 2**exponent).astype(jnp.int32)
    gap_depth = jnp.maximum(node_depth[None, :] - node_depth[:, None], 0)
    ancestor = (node_depth[:, None] < node_depth[None, :]) & (
        jnp.right_shift(heap_label[None, :], gap_depth) == heap_label[:, None]
    )
    return (node_of, node_depth, ancestor)


def lookup(source, indices, length):
    hits = indices[:, None] == jnp.arange(length, dtype=jnp.int32)[None, :]
    return jnp.sum(jnp.where(hits, source[None, :], 0), axis=1)


def rows_from_columns(factor, vector, weights):
    blocks = lax.dot_general(
        vector, factor, (((2,), (3,)), ((1,), (2,))), preferred_element_type=jnp.float32
    )
    return jnp.sum(weights.T[:, None, :, None] * blocks, axis=0)


def columns_from_rows(factor, vector, weights):
    blocks = lax.dot_general(
        vector, factor, (((2,), (1,)), ((1,), (0,))), preferred_element_type=jnp.float32
    )
    return jnp.sum(weights[:, None, :, None] * blocks, axis=0)


def to_columns(vector):
    row_count = lax.axis_size("prow")
    col_count = lax.axis_size("pcol")
    row_groups = row_count // col_count
    col_index = lax.axis_index("pcol")
    rhs_count, row_tiles, tile_rows = vector.shape
    collected = lax.all_gather(vector, "prow", axis=1, tiled=True)
    collected = collected.reshape(rhs_count, row_groups, col_count, row_tiles, tile_rows)
    picked = lax.dynamic_index_in_dim(collected, col_index, 2, keepdims=False)
    return jnp.transpose(picked, (0, 2, 1, 3)).reshape(rhs_count, row_tiles * row_groups, tile_rows)


def to_rows(vector):
    row_count = lax.axis_size("prow")
    col_count = lax.axis_size("pcol")
    row_groups = row_count // col_count
    row_index = lax.axis_index("prow")
    rhs_count, col_tiles, tile_rows = vector.shape
    shaped = vector.reshape(rhs_count, col_tiles // row_groups, row_groups, tile_rows)
    chosen = lax.dynamic_index_in_dim(shaped, row_index // col_count, 2, keepdims=False)
    collected = lax.all_gather(chosen, "pcol", axis=1, tiled=True)
    collected = collected.reshape(rhs_count, col_count, col_tiles // row_groups, tile_rows)
    return lax.dynamic_index_in_dim(collected, row_index % col_count, 1, keepdims=False)


def sum_rows(partial_value):
    return lax.psum(partial_value, "pcol")


def sum_cols(partial_value):
    return lax.psum(partial_value, "prow")


def shards(right_sides, factor, node_sizes, row_blocks):
    row_count = lax.axis_size("prow")
    col_count = lax.axis_size("pcol")
    row_index = lax.axis_index("prow")
    col_index = lax.axis_index("pcol")
    row_tiles = factor.shape[0]
    col_tiles = factor.shape[2]
    rhs_count = right_sides.shape[0]
    tile_rows = right_sides.shape[2]
    node_count = node_sizes.shape[0]
    tile_count = row_blocks.shape[1]
    node_of, node_depth, ancestor = tree_tables(node_sizes, row_blocks)
    mine_rows = jnp.arange(row_tiles, dtype=jnp.int32) * row_count + row_index
    mine_cols = jnp.arange(col_tiles, dtype=jnp.int32) * col_count + col_index
    owner_rows = lookup(node_of, mine_rows, tile_count)
    owner_cols = lookup(node_of, mine_cols, tile_count)
    depth_rows = lookup(node_depth, owner_rows, node_count)
    depth_cols = lookup(node_depth, owner_cols, node_count)
    node_ids = jnp.arange(node_count, dtype=jnp.int32)
    hits_rows = owner_rows[:, None] == node_ids[None, :]
    hits_cols = owner_cols[:, None] == node_ids[None, :]
    above = jnp.any(
        hits_rows[:, None, :, None] & ancestor[None, None, :, :] & hits_cols[None, :, None, :],
        axis=(2, 3),
    )
    tile_hits = mine_rows[:, None] == jnp.arange(tile_count, dtype=jnp.int32)[None, :]
    flagged = jnp.any(
        tile_hits[:, None, None, :]
        & hits_cols[None, :, :, None]
        & (row_blocks == 1)[None, None, :, :],
        axis=(2, 3),
    )
    diagonal = owner_rows[:, None] == owner_cols[None, :]
    linked = above & flagged
    correction = jnp.zeros(right_sides.shape, jnp.float32)
    forward = jnp.zeros(right_sides.shape, jnp.float32)
    forward_cols = jnp.zeros((rhs_count, col_tiles, tile_rows), jnp.float32)
    for height in range(LEVELS - 1, -1, -1):
        at_rows = depth_rows == height
        at_cols = depth_cols == height
        current = (right_sides - correction).astype(jnp.bfloat16)
        solve_weights = (diagonal & at_rows[:, None]).astype(jnp.float32)
        solved = sum_rows(rows_from_columns(factor, to_columns(current), solve_weights))
        forward = forward + solved
        solved_cols = to_columns(solved.astype(jnp.bfloat16))
        forward_cols = forward_cols + solved_cols.astype(jnp.float32)
        if height > 0:
            update_weights = (linked & at_cols[None, :]).astype(jnp.float32)
            correction = correction + sum_rows(
                rows_from_columns(factor, solved_cols, update_weights)
            )
    solution = jnp.zeros((rhs_count, col_tiles, tile_rows), jnp.float32)
    correction_cols = jnp.zeros((rhs_count, col_tiles, tile_rows), jnp.float32)
    for height in range(LEVELS):
        at_rows = depth_rows == height
        at_cols = depth_cols == height
        if height == 0:
            current = forward.astype(jnp.bfloat16)
        else:
            current = to_rows((forward_cols - correction_cols).astype(jnp.bfloat16))
        solve_weights = (diagonal & at_cols[None, :]).astype(jnp.float32)
        solved = sum_cols(columns_from_rows(factor, current, solve_weights))
        solution = solution + solved
        if height < LEVELS - 1:
            solved_rows = to_rows(solved.astype(jnp.bfloat16))
            update_weights = (linked & at_rows[:, None]).astype(jnp.float32)
            correction_cols = correction_cols + sum_cols(
                columns_from_rows(factor, solved_rows, update_weights)
            )
    return (forward, solution)


def solution(mesh):
    in_specs = (P(None, None, "prow"), P(None, "prow", None, "pcol"), P(), P())
    out_specs = (P(None, None, "prow"), P(None, None, "pcol"))
    return jax.shard_map(shards, mesh=mesh, in_specs=in_specs, out_specs=out_specs, check_vma=False)
```

profile of v0, /device:TPU:0, one launch (start us, length us, event | category | flops | bytes accessed | tf_op | source)
XLA Modules:
  0.0 793.3 jit_solution(14260200867232302940)
XLA Ops:
  7.2 0.0 copy-start
  7.2 0.0 copy-start.3
  7.2 0.0 all-reduce.6.cloned.1.call-start
  7.3 0.9 reduce-window.8
  8.2 0.1 convert_reduce_fusion
  8.3 0.6 select_reduce_fusion.3
  8.9 0.6 iota_compare_fusion.3
  9.5 1.3 select_reduce_fusion.2
  12.1 0.2 select_reduce_fusion.1
  12.3 0.1 iota_compare_fusion
  12.4 0.1 copy.64
  12.5 0.2 select_reduce_fusion
  12.7 0.1 fusion.28
  12.8 0.1 and_reduce_fusion.1
  12.9 0.5 copy-done.4
  13.4 0.6 and_convert_fusion.4
  14.7 43.8 %all_gather.30 = bf16[32,16,256]{2,0,1:T(8,128)(2,1)S(1)} all-gather(bf16[32,1,256]{2,0,1:T(8,128)(2,1)S(1)} %copy.112), channel_id=1, replica_groups=mesh['prow'=16,'pcol'=2] {'prow'}, dimensions={1}, use_global_device_ids=true | all-gather | bytes 278528 | tf_op jit(solution)/shard_map/all_gather | solution.py:51
  58.5 0.2 and_reduce_fusion
  58.7 0.4 fusion
  59.2 3.4 psum.70
  62.6 36.9 %all_gather.31 = bf16[32,16,256]{2,0,1:T(8,128)(2,1)S(1)} all-gather(bf16[32,1,256]{2,0,1:T(8,128)(2,1)S(1)} %convert_element_type.179), channel_id=1, replica_groups=mesh['prow'=16,'pcol'=2] {'prow'}, dimensions={1}, use_global_device_ids=true | all-gather | bytes 278528 | tf_op jit(solution)/shard_map/all_gather | solution.py:51
  99.4 0.4 fusion.1
  99.9 3.4 psum.71
  103.3 38.9 %all_gather.32 = bf16[32,16,256]{2,0,1:T(8,128)(2,1)S(1)} all-gather(bf16[32,1,256]{2,0,1:T(8,128)(2,1)S(1)} %subtract_convert_fusion.2), channel_id=1, replica_groups=mesh['prow'=16,'pcol'=2] {'prow'}, dimensions={1}, use_global_device_ids=true | all-gather | bytes 278528 | tf_op jit(solution)/shard_map/all_gather | solution.py:51
  142.2 0.4 fusion.2
  142.6 3.4 psum.72
  146.1 36.9 %all_gather.33 = bf16[32,16,256]{2,0,1:T(8,128)(2,1)S(1)} all-gather(bf16[32,1,256]{2,0,1:T(8,128)(2,1)S(1)} %convert_element_type.183), channel_id=1, replica_groups=mesh['prow'=16,'pcol'=2] {'prow'}, dimensions={1}, use_global_device_ids=true | all-gather | bytes 278528 | tf_op jit(solution)/shard_map/all_gather | solution.py:51
  182.9 0.4 fusion.3
  183.4 3.4 psum.73
  186.8 39.0 %all_gather.34 = bf16[32,16,256]{2,0,1:T(8,128)(2,1)S(1)} all-gather(bf16[32,1,256]{2,0,1:T(8,128)(2,1)S(1)} %subtract_convert_fusion.1), channel_id=1, replica_groups=mesh['prow'=16,'pcol'=2] {'prow'}, dimensions={1}, use_global_device_ids=true | all-gather | bytes 278528 | tf_op jit(solution)/shard_map/all_gather | solution.py:51
  225.8 0.4 fusion.4
  226.2 3.4 psum.74
  229.6 1.0 convolution_multiply_fusion.4
  230.6 0.0 all-reduce.6.cloned.1.call-update
  230.6 0.0 all-reduce.8.cloned.1.call-start
  230.7 104.0 %all-reduce.6.cloned.1.call-done = f32[32,8,256]{2,0,1:T(8,128)} async-done(((f32[32,8,256]{2,0,1:T(8,128)}), f32[32,8,256]{2,0,1:T(8,128)}) %all-reduce.6.cloned.1.call-update) | async-done | bytes 262160 | tf_op jit(solution)/shard_map/psum | solution.py:75
  334.7 0.8 dynamic-slice_convert_fusion.1
  335.5 1.8 all_gather.36
  337.3 1.0 convolution_multiply_fusion.3
  338.3 0.0 all-reduce.8.cloned.1.call-update
  338.3 0.0 all-reduce.10.cloned.1.call-start
  338.3 40.2 %all_gather.35 = bf16[32,16,256]{2,0,1:T(8,128)(2,1)S(1)} all-gather(bf16[32,1,256]{2,0,1:T(8,128)(2,1)S(1)} %get-tuple-element.14), channel_id=1, replica_groups=mesh['prow'=16,'pcol'=2] {'prow'}, dimensions={1}, use_global_device_ids=true | all-gather | bytes 278528 | tf_op jit(solution)/shard_map/all_gather | solution.py:51
  378.6 0.1 convert_add_fusion
  378.6 68.9 %all-reduce.8.cloned.1.call-done = f32[32,8,256]{2,0,1:T(8,128)} async-done(((f32[32,8,256]{2,0,1:T(8,128)}), f32[32,8,256]{2,0,1:T(8,128)}) %all-reduce.8.cloned.1.call-update) | async-done | bytes 262160 | tf_op jit(solution)/shard_map/psum | solution.py:75
  447.5 0.8 subtract_convert_fusion
  448.3 1.8 all_gather.37
  450.1 1.0 convolution_multiply_fusion.2
  451.1 0.0 all-reduce.10.cloned.1.call-update
  451.1 0.0 all-reduce.12.cloned.1.call-start
  451.2 108.9 %all-reduce.10.cloned.1.call-done = f32[32,8,256]{2,0,1:T(8,128)} async-done(((f32[32,8,256]{2,0,1:T(8,128)}), f32[32,8,256]{2,0,1:T(8,128)}) %all-reduce.10.cloned.1.call-update) | async-done | bytes 262160 | tf_op jit(solution)/shard_map/psum | solution.py:75
  560.1 0.8 dynamic-slice_convert_fusion
  560.8 1.8 all_gather.38
  562.7 1.0 convolution_multiply_fusion.1
  563.6 0.0 all-reduce.12.cloned.1.call-update
  563.7 0.0 all-reduce.14.cloned.1.call-start
  563.7 108.7 %all-reduce.12.cloned.1.call-done = f32[32,8,256]{2,0,1:T(8,128)} async-done(((f32[32,8,256]{2,0,1:T(8,128)}), f32[32,8,256]{2,0,1:T(8,128)}) %all-reduce.12.cloned.1.call-update) | async-done | bytes 262160 | tf_op jit(solution)/shard_map/psum | solution.py:75
  672.5 0.8 fusion.16
  673.3 1.8 all_gather.39
  675.1 1.0 convolution_multiply_fusion
  676.1 0.0 all-reduce.14.cloned.1.call-update
  676.1 0.6 copy.81
  676.8 108.1 %all-reduce.14.cloned.1.call-done = f32[32,8,256]{2,0,1:T(8,128)} async-done(((f32[32,8,256]{2,0,1:T(8,128)}), f32[32,8,256]{2,0,1:T(8,128)}) %all-reduce.14.cloned.1.call-update) | async-done | bytes 262160 | tf_op jit(solution)/shard_map/psum | solution.py:75
  784.9 1.0 add_add_fusion
  785.9 0.9 copy.82
  (19 shorter events, 0.1 us)
Async XLA Ops:
  7.2 51.5 %copy-start = (bf16[1,256,8,256]{3,2,1,0:T(8,128)(2,1)S(1)}, bf16[1,256,8,256]{3,2,1,0:T(8,128)(2,1)}, u32[]{:S(2)}) copy-start(bf16[1,256,8,256]{3,2,1,0:T(8,128)(2,1)} %param.5) | copy-start | bytes 3145732
  7.2 7.5 copy-start.3
  7.2 327.5 %all-reduce.6.cloned.1.call-start = ((), (), s32[]{:S(2)}) async-start(), calls=%async_computation | async-start | bytes 524288 | tf_op jit(solution)/shard_map/psum | solution.py:75
  12.7 0.7 copy-start.4
  230.6 216.9 %all-reduce.8.cloned.1.call-start = ((), (), s32[]{:S(2)}) async-start(), calls=%async_computation.1 | async-start | bytes 524288 | tf_op jit(solution)/shard_map/psum | solution.py:75
  338.3 221.8 %all-reduce.10.cloned.1.call-start = ((), (), s32[]{:S(2)}) async-start(), calls=%async_computation.2 | async-start | bytes 524288 | tf_op jit(solution)/shard_map/psum | solution.py:75
  451.1 221.4 %all-reduce.12.cloned.1.call-start = ((), (), s32[]{:S(2)}) async-start(), calls=%async_computation.3 | async-start | bytes 524288 | tf_op jit(solution)/shard_map/psum | solution.py:75
  563.7 221.2 %all-reduce.14.cloned.1.call-start = ((), (), s32[]{:S(2)}) async-start(), calls=%async_computation.4 | async-start | bytes 524288 | tf_op jit(solution)/shard_map/psum | solution.py:75
  675.1 109.8 %copy-start.2 = (f32[32,8,256]{2,0,1:T(8,128)S(1)}, f32[32,8,256]{2,0,1:T(8,128)}, u32[]{:S(2)}) copy-start(f32[32,8,256]{2,0,1:T(8,128)} %all-reduce.10.cloned.1.call-done) | copy-start | bytes 786436
  676.1 108.8 %copy-start.1 = (f32[32,8,256]{2,0,1:T(8,128)S(1)}, f32[32,8,256]{2,0,1:T(8,128)}, u32[]{:S(2)}) copy-start(f32[32,8,256]{2,0,1:T(8,128)} %all-reduce.6.cloned.1.call-done) | copy-start | bytes 786436
Sparse Core Ops, SparseCore 0:
  230.8 103.9 all-reduce.5
  340.5 106.9 all-reduce.7
  453.3 106.7 all-reduce.9
  565.7 106.6 all-reduce.11
  678.1 106.7 all-reduce.13
where the time goes:
time: 794 us; the launch traced here: 793 us
  waiting for transfers between devices  499 us (63%)
  blocking collectives  260 us (33%)
  between operations  16 us (2%)
    psum x5, waiting for transfers between devices, sum_cols(): return lax.psum(partial_value, 'prow')  499 us
    all_gather x6, blocking collectives, to_columns(): collected = lax.all_gather(vector, 'prow', axis=1, tiled=True)  236 us
    psum x5, blocking collectives, sum_rows(): return lax.psum(partial_value, 'pcol')  17 us
  transfers between devices with their start and end apart: 5, of which 5 were waited for; matrix products, arithmetic and copies ran while one was open for 0% of the time, Pallas kernels for 0%

commit v1 on v0

--- a/solution.py
+++ b/solution.py
@@ -72,7 +72,7 @@
 
 
 def sum_cols(partial_value):
-    return lax.psum(partial_value, "prow")
+    return jnp.sum(lax.all_gather(partial_value, "prow"), axis=0)
 
 
 def shards(right_sides, factor, node_sizes, row_blocks):

time: 794 us -> 638 us (0.80)
  waiting for transfers between devices: 499 us -> 332 us
  other arithmetic: 7.72 us -> 19.3 us
    psum x5 -> x0, waiting for transfers between devices: 499 us -> none  [sum_cols(): return lax.psum(partial_value, 'prow')]
    all_gather x0 -> x5, waiting for transfers between devices: none -> 332 us  [sum_cols(): return jnp.sum(lax.all_gather(partial_value, 'prow'), axis=0)]
    reduce_sum x0 -> x5, other arithmetic: none -> 12.5 us  [sum_cols(): return jnp.sum(lax.all_gather(partial_value, 'prow'), axis=0)]
where the time goes in v1:
time: 638 us; the launch traced here: 637 us
  waiting for transfers between devices  332 us (52%)
  blocking collectives  260 us (41%)
  other arithmetic  19.3 us (3%)
  between operations  16 us (3%)
  matrix products  7.07 us (1%)
    all_gather x5, waiting for transfers between devices, sum_cols(): return jnp.sum(lax.all_gather(partial_value, 'prow'), axis=0)  332 us
    all_gather x6, blocking collectives, to_columns(): collected = lax.all_gather(vector, 'prow', axis=1, tiled=True)  235 us
    psum x5, blocking collectives, sum_rows(): return lax.psum(partial_value, 'pcol')  17 us
  transfers between devices with their start and end apart: 5, of which 5 were waited for; matrix products, arithmetic and copies ran while one was open for 0% of the time, Pallas kernels for 0%

profile of v1, /device:TPU:0, one launch (start us, length us, event | category | flops | bytes accessed | tf_op | source)
XLA Modules:
  0.0 636.8 jit_solution(6909736138122105296)
XLA Ops:
  7.2 0.0 all-gather.11.cloned.1.call-start
  7.3 0.9 reduce-window.8
  8.2 0.1 convert_reduce_fusion
  8.2 0.6 select_reduce_fusion.3
  8.9 1.3 select_reduce_fusion.2
  11.5 0.7 iota_compare_fusion.3
  12.8 0.2 select_reduce_fusion.1
  13.0 0.1 iota_compare_fusion
  13.1 0.1 copy.63
  13.2 0.7 broadcast_compare_fusion
  13.8 0.2 select_reduce_fusion
  14.0 0.1 fusion.28
  14.1 0.1 and_reduce_fusion.1
  14.2 0.7 and_convert_fusion.4
  14.9 0.8 copy.111
  15.7 43.8 %all_gather.50 = bf16[32,16,256]{2,0,1:T(8,128)(2,1)S(1)} all-gather(bf16[32,1,256]{2,0,1:T(8,128)(2,1)S(1)} %copy.111), channel_id=1, replica_groups=mesh['prow'=16,'pcol'=2] {'prow'}, dimensions={1}, use_global_device_ids=true | all-gather | bytes 278528 | tf_op jit(solution)/shard_map/all_gather | solution.py:51
  59.4 0.2 and_reduce_fusion
  59.7 0.4 fusion
  60.1 3.4 psum.35
  63.5 36.9 %all_gather.51 = bf16[32,16,256]{2,0,1:T(8,128)(2,1)S(1)} all-gather(bf16[32,1,256]{2,0,1:T(8,128)(2,1)S(1)} %convert_element_type.179), channel_id=1, replica_groups=mesh['prow'=16,'pcol'=2] {'prow'}, dimensions={1}, use_global_device_ids=true | all-gather | bytes 278528 | tf_op jit(solution)/shard_map/all_gather | solution.py:51
  100.4 0.4 fusion.1
  100.8 3.4 psum.36
  104.2 0.8 subtract_convert_fusion.2
  105.0 38.9 %all_gather.52 = bf16[32,16,256]{2,0,1:T(8,128)(2,1)S(1)} all-gather(bf16[32,1,256]{2,0,1:T(8,128)(2,1)S(1)} %subtract_convert_fusion.2), channel_id=1, replica_groups=mesh['prow'=16,'pcol'=2] {'prow'}, dimensions={1}, use_global_device_ids=true | all-gather | bytes 278528 | tf_op jit(solution)/shard_map/all_gather | solution.py:51
  143.9 0.4 fusion.2
  144.3 3.4 psum.37
  147.8 36.9 %all_gather.53 = bf16[32,16,256]{2,0,1:T(8,128)(2,1)S(1)} all-gather(bf16[32,1,256]{2,0,1:T(8,128)(2,1)S(1)} %convert_element_type.183), channel_id=1, replica_groups=mesh['prow'=16,'pcol'=2] {'prow'}, dimensions={1}, use_global_device_ids=true | all-gather | bytes 278528 | tf_op jit(solution)/shard_map/all_gather | solution.py:51
  184.6 0.4 fusion.3
  185.1 3.4 psum.38
  188.5 39.0 %all_gather.54 = bf16[32,16,256]{2,0,1:T(8,128)(2,1)S(1)} all-gather(bf16[32,1,256]{2,0,1:T(8,128)(2,1)S(1)} %subtract_convert_fusion.1), channel_id=1, replica_groups=mesh['prow'=16,'pcol'=2] {'prow'}, dimensions={1}, use_global_device_ids=true | all-gather | bytes 278528 | tf_op jit(solution)/shard_map/all_gather | solution.py:51
  227.5 0.4 fusion.4
  227.9 3.4 psum.39
  231.3 1.0 convolution_multiply_fusion.4
  232.3 0.0 all-gather.11.cloned.1.call-update
  232.3 0.0 all-gather.13.cloned.1.call-start
  232.4 72.4 %all-gather.11.cloned.1.call-done = f32[512,8,256]{2,0,1:T(8,128)} async-done(((f32[32,8,256]{2,0,1:T(8,128)}), f32[512,8,256]{2,0,1:T(8,128)}) %all-gather.11.cloned.1.call-update) | async-done | bytes 4194320 | tf_op jit(solution)/shard_map/all_gather | solution.py:75
  304.8 2.5 reduce_sum.180
  307.3 1.8 all_gather.57
  309.2 1.0 convolution_multiply_fusion.3
  310.2 0.0 all-gather.13.cloned.1.call-update
  310.2 0.0 all-gather.15.cloned.1.call-start
  310.2 40.1 %all_gather.56 = bf16[32,16,256]{2,0,1:T(8,128)(2,1)S(1)} all-gather(bf16[32,1,256]{2,0,1:T(8,128)(2,1)S(1)} %get-tuple-element.12), channel_id=1, replica_groups=mesh['prow'=16,'pcol'=2] {'prow'}, dimensions={1}, use_global_device_ids=true | all-gather | bytes 278528 | tf_op jit(solution)/shard_map/all_gather | solution.py:51
  350.4 0.1 convert_add_fusion
  350.4 35.7 %all-gather.13.cloned.1.call-done = f32[512,8,256]{2,0,1:T(8,128)} async-done(((f32[32,8,256]{2,0,1:T(8,128)}), f32[512,8,256]{2,0,1:T(8,128)}) %all-gather.13.cloned.1.call-update) | async-done | bytes 4194320 | tf_op jit(solution)/shard_map/all_gather | solution.py:75
  386.1 2.5 reduce_sum.181
  388.7 1.8 all_gather.59
  390.5 1.0 convolution_multiply_fusion.2
  391.5 0.0 all-gather.15.cloned.1.call-update
  391.5 0.0 all-gather.17.cloned.1.call-start
  391.5 74.8 %all-gather.15.cloned.1.call-done = f32[512,8,256]{2,0,1:T(8,128)} async-done(((f32[32,8,256]{2,0,1:T(8,128)}), f32[512,8,256]{2,0,1:T(8,128)}) %all-gather.15.cloned.1.call-update) | async-done | bytes 4194320 | tf_op jit(solution)/shard_map/all_gather | solution.py:75
  466.4 2.5 reduce_sum.182
  468.9 1.8 all_gather.61
  470.7 1.0 convolution_multiply_fusion.1
  471.7 0.0 all-gather.17.cloned.1.call-update
  471.7 0.0 all-gather.19.cloned.1.call-start
  471.8 74.8 %all-gather.17.cloned.1.call-done = f32[512,8,256]{2,0,1:T(8,128)} async-done(((f32[32,8,256]{2,0,1:T(8,128)}), f32[512,8,256]{2,0,1:T(8,128)}) %all-gather.17.cloned.1.call-update) | async-done | bytes 4194320 | tf_op jit(solution)/shard_map/all_gather | solution.py:75
  546.6 2.5 reduce_sum.183
  549.1 1.8 all_gather.63
  551.0 1.0 convolution_multiply_fusion
  552.0 0.6 copy.80
  552.6 74.2 %all-gather.19.cloned.1.call-done = f32[512,8,256]{2,0,1:T(8,128)} async-done(((f32[32,8,256]{2,0,1:T(8,128)}), f32[512,8,256]{2,0,1:T(8,128)}) %all-gather.19.cloned.1.call-update) | async-done | bytes 4194320 | tf_op jit(solution)/shard_map/all_gather | solution.py:75
  626.8 2.5 reduce_sum.184
  629.4 0.1 add_add_fusion
  629.4 0.9 copy.81
  (18 shorter events, 0.2 us)
Async XLA Ops:
  7.2 52.5 %copy-start = (bf16[1,256,8,256]{3,2,1,0:T(8,128)(2,1)S(1)}, bf16[1,256,8,256]{3,2,1,0:T(8,128)(2,1)}, u32[]{:S(2)}) copy-start(bf16[1,256,8,256]{3,2,1,0:T(8,128)(2,1)} %param.5) | copy-start | bytes 3145732
  7.2 181.3 %copy-start.1 = (f32[32,1,256]{2,1,0:T(1,128)S(1)}, f32[32,1,256]{2,1,0:T(1,128)}, u32[]{:S(2)}) copy-start(f32[32,1,256]{2,1,0:T(1,128)} %param.4) | copy-start | bytes 98308
  7.2 297.6 %all-gather.11.cloned.1.call-start = ((), (), s32[]{:S(2)}) async-start(), calls=%async_computation | async-start | bytes 4456448 | tf_op jit(solution)/shard_map/all_gather | solution.py:75
  232.3 153.8 %all-gather.13.cloned.1.call-start = ((), (), s32[]{:S(2)}) async-start(), calls=%async_computation.1 | async-start | bytes 4456448 | tf_op jit(solution)/shard_map/all_gather | solution.py:75
  310.2 156.2 %all-gather.15.cloned.1.call-start = ((), (), s32[]{:S(2)}) async-start(), calls=%async_computation.2 | async-start | bytes 4456448 | tf_op jit(solution)/shard_map/all_gather | solution.py:75
  391.5 155.1 %all-gather.17.cloned.1.call-start = ((), (), s32[]{:S(2)}) async-start(), calls=%async_computation.3 | async-start | bytes 4456448 | tf_op jit(solution)/shard_map/all_gather | solution.py:75
  471.7 155.1 %all-gather.19.cloned.1.call-start = ((), (), s32[]{:S(2)}) async-start(), calls=%async_computation.4 | async-start | bytes 4456448 | tf_op jit(solution)/shard_map/all_gather | solution.py:75
Sparse Core Ops, SparseCore 0:
  232.5 72.3 all-gather.10
  310.3 75.7 all-gather.12
  391.6 74.6 all-gather.14
  471.9 74.6 all-gather.16
  552.1 74.6 all-gather.18
